TPU v7x, 32 devices: a whole 2x2x4 slice. The times are simulated.
32 devices in a mesh: ctx: 4 (over y, x), head: 8 (over z, core).
Axes of the slice: x: 2, y: 2, z: 4, core: 2. Of those that a mesh axis runs over, the one named last changes fastest.
Arguments:
- queries: bfloat16 [4096, 8192], P('ctx', 'head'), may hold values from -12 to 12
- key_heads: bfloat16 [1024, 4096], P(None, 'ctx'), may hold values from -6 to 6
- value_heads: bfloat16 [1024, 4096], P(None, 'ctx'), may hold values from -6 to 6
- out_weight: bfloat16 [8192, 8192], P('head'), may hold values from -0.09375 to 0.09375
- block_order: int32 [8], replicated, may hold values from 0 to 7, each once
- doc_ids: int32 [4096], replicated, may hold values from 0 to 5, never falling along the last dimension, each value on 1 to 1024 neighbouring positions
Outputs:
- projected: bfloat16 [4096, 8192], P('ctx', 'head')
Inputs may be any that keep to these rules, and one draw needn't show every extreme that they name: Layout slot j (rows j * 512 to (j + 1) * 512 - 1 of queries and projected, the same columns of key_heads and value_heads) holds block block_order[j] of the sequence; each of 0 to 7 appears once. `doc_ids`: ids never fall along the sequence; every id is used; each document holds 1 to 1024 tokens and one holds exactly 1024.
All inputs are finite; a program needn't handle non-finite values.
Results may differ from a plain program's by a relative error of at most 0.014.
Values may be sent and summed in bfloat16 or wider, within the bound.
No kernel may reach another device: no remote copies, remote signals or barrier semaphores. Data moves between devices by JAX's collectives and lax.ppermute only.
A program may use at most 192 MiB of HBM per device.

v0:
```python
import jax
import jax.numpy as jnp
from jax import lax
from jax.sharding import PartitionSpec as P

KVH = 8
HD = 128
floor_score = -1e30


def locate(row_ids, block_order, doc_ids):
    block_len = doc_ids.shape[0] // block_order.shape[0]
    block_id = row_ids // block_len
    slot_table = jnp.arange(block_order.shape[0], dtype=jnp.int32)
    starts = jnp.sum(
        jnp.where(block_id[:, None] == slot_table[None, :], block_order[None, :], 0), axis=1
    )
    places = starts * block_len + row_ids % block_len
    return (places, jnp.take(doc_ids, places))


def attend_block(
    running, key_block, value_block, key_place, key_doc, query_heads, query_place, query_doc
):
    visible = (key_place[None, :] <= query_place[:, None]) & (
        key_doc[None, :] == query_doc[:, None]
    )
    row_top, row_total, row_accum = running
    scores = jnp.einsum(
        "thd,dk->thk", query_heads, key_block, preferred_element_type=jnp.float32
    ) * key_block.shape[0] ** (-0.5)
    scores = jnp.where(visible[:, None, :], scores, floor_score)
    new_top = jnp.maximum(row_top, jnp.max(scores, axis=2))
    factor = jnp.exp(row_top - new_top)
    weights = jnp.where(visible[:, None, :], jnp.exp(scores - new_top[:, :, None]), 0.0)
    row_total = row_total * factor + jnp.sum(weights, axis=2)
    mixed = jnp.einsum(
        "thk,dk->thd", weights.astype(jnp.bfloat16), value_block, preferred_element_type=jnp.float32
    )
    row_accum = row_accum * factor[:, :, None] + mixed
    return (new_top, row_total, row_accum)


def attend_span(
    running, key_piece, value_piece, query_heads, query_place, query_doc, block_order, doc_ids
):
    key_count = key_piece.shape[1]
    block_width = 1024
    rounds = key_count // block_width
    places, doc_list = locate(jnp.arange(key_count, dtype=jnp.int32), block_order, doc_ids)

    def one_round(round_index, current):
        offset = round_index * block_width
        return attend_block(
            current,
            lax.dynamic_slice_in_dim(key_piece, offset, block_width, 1),
            lax.dynamic_slice_in_dim(value_piece, offset, block_width, 1),
            lax.dynamic_slice_in_dim(places, offset, block_width, 0),
            lax.dynamic_slice_in_dim(doc_list, offset, block_width, 0),
            query_heads,
            query_place,
            query_doc,
        )

    return lax.fori_loop(0, rounds, one_round, running)


def normalize(running, row_count):
    row_top, row_total, row_accum = running
    return (row_accum / row_total[:, :, None]).astype(jnp.bfloat16).reshape(row_count, -1)


def shards(queries, key_heads, value_heads, out_weight, block_order, doc_ids):
    row_count = queries.shape[0]
    head_count = queries.shape[1] // HD
    group_size = lax.axis_size("head") // KVH
    lane_index = lax.axis_index("head")
    kv_start = lane_index // group_size * HD
    key_part = lax.dynamic_slice_in_dim(key_heads, kv_start, HD, 0)
    value_part = lax.dynamic_slice_in_dim(value_heads, kv_start, HD, 0)
    ctx_index = lax.axis_index("ctx")
    own_rows = ctx_index * row_count + jnp.arange(row_count, dtype=jnp.int32)
    query_place, query_doc = locate(own_rows, block_order, doc_ids)
    query_heads = queries.reshape(row_count, head_count, HD)
    running = attend_span(
        (
            jnp.full((row_count, head_count), floor_score, jnp.float32),
            jnp.zeros((row_count, head_count), jnp.float32),
            jnp.zeros((row_count, head_count, HD), jnp.float32),
        ),
        lax.all_gather(key_part, "ctx", axis=1, tiled=True),
        lax.all_gather(value_part, "ctx", axis=1, tiled=True),
        query_heads,
        query_place,
        query_doc,
        block_order,
        doc_ids,
    )
    context = normalize(running, row_count)
    partial_sum = jnp.dot(context, out_weight, preferred_element_type=jnp.float32)
    return lax.psum_scatter(
        partial_sum.astype(jnp.bfloat16), "head", scatter_dimension=1, tiled=True
    )


def solution(mesh):
    placed = (P("ctx", "head"), P(None, "ctx"), P(None, "ctx"), P("head", None), P(), P())
    return jax.shard_map(
        shards, mesh=mesh, in_specs=placed, out_specs=P("ctx", "head"), check_vma=False
    )
```

profile of v0, /device:TPU:0, one launch (start us, length us, event | category | flops | bytes accessed | tf_op | source)
XLA Modules:
  0.0 472.5 jit_solution(731710215248140285)
XLA Ops:
  6.5 0.0 copy-start
  6.5 0.0 copy-start.2
  6.5 0.0 all-gather.3.cloned.1.call-start
  6.5 1.6 copy-done
  8.1 0.8 copy.20
  9.0 0.0 all-gather.3.cloned.1.call-update
  9.0 0.0 all-gather.5.cloned.1.call-start
  9.0 1.7 constant_dynamic-slice_fusion.1
  10.7 0.0 all-gather.5.cloned.1.call-update
  10.8 0.0 reduce-scatter.2.cloned.1.call-start
  10.8 0.7 select_reduce_fusion.1
  11.6 0.8 select_reduce_fusion
  12.4 5.8 %gather_fusion.1 = s32[1024]{0:T(1024)S(1)} fusion(s32[4096]{0:T(1024)} %param.13, s32[1024]{0:T(1024)S(1)} %broadcast_clamp_fusion.1), kind=kCustom, calls=%fused_computation.1 | custom fusion | bytes 12288 | tf_op jit(solution)/shard_map/jit(_take)/gather | solution.py:19
  18.3 0.0 copy-done.2
  18.3 23.0 %gather_fusion = s32[4096]{0:T(1024)S(1)} fusion(s32[4096]{0:T(1024)S(1)} %copy-done.2, s32[4096]{0:T(1024)S(1)} %broadcast_clamp_fusion), kind=kCustom, calls=%fused_computation | custom fusion | bytes 49152 | tf_op jit(solution)/shard_map/jit(_take)/gather | solution.py:19
  41.3 2.9 copy.16
  44.2 2.4 copy.17
  46.6 0.0 all-gather.3.cloned.1.call-done
  46.6 20.5 %all-gather.5.cloned.1.call-done = bf16[128,4096]{1,0:T(8,128)(2,1)} async-done(((bf16[128,1024]{1,0:T(8,128)(2,1)}), bf16[128,4096]{1,0:T(8,128)(2,1)}) %all-gather.5.cloned.1.call-update) | async-done | bytes 1048592 | tf_op jit(solution)/shard_map/all_gather | solution.py:92
  67.1 196.0 %while.18 = (s32[]{:T(128)}, f32[1024,8]{0,1:T(8,128)S(1)}, f32[1024,8]{0,1:T(8,128)S(1)}, f32[1024,8,128]{2,0,1:T(8,128)}, s32[4096]{0:T(1024)S(1)}, /*index=5*...) while((s32[]{:T(128)}, f32[1024,8]{0,1:T(8,128)S(1)}, ...), condition=%wide.region_5.6_spmd.clone, body=%wide.region_2.5_spmd.clone.sunk | while | flops 4410351616 | bytes 116424928 | solution.py:65
  67.1 1.2 compare_and_fusion.2
  68.2 14.9 %fusion.51 = (f32[1024,8]{0,1:T(8,128)S(1)}, f32[1024,1024,8]{1,0,2:T(8,128)}) fusion(pred[1024,1024]{0,1:T(8,128)(4,1)S(1)} %compare_and_fusion.2, bf16[1024,8,128]{2,0,1:T(8,128)(2,1)} %get-tuple-element.394, bf16[128,4096]{0,1:T(8,128)(2,1)} %get-tuple-element.393, s32[]{:T(128)S(6)} %select_n.212), kind=kOutput, calls=%fused_computation.4.clone.1 | convolution fusion | flops 2172641280 | bytes 36995076 | tf_op jit(solution)/shard_map/while/body/eval_jaxpr/thd,dk->thk/dot_general | solution.py:29
  83.1 14.7 %fusion.52 = f32[1024,8]{0,1:T(8,128)S(1)} fusion(f32[1024,1024,8]{1,0,2:T(8,128)} %get-tuple-element.352, f32[1024,8]{0,1:T(8,128)S(1)} %select_maximum_fusion.2, pred[1024,1024]{0,1:T(8,128)(4,1)S(1)} %compare_and_fusion.2), kind=kLoop, calls=%fused_computation.6.clone.1 | loop fusion | flops 41934848 | bytes 34668544 | tf_op jit(solution)/shard_map/while/body/eval_jaxpr/reduce_sum | solution.py:36
  97.9 17.4 %fusion.54 = f32[1024,8,128]{2,0,1:T(8,128)} fusion(f32[1024,8,128]{2,0,1:T(8,128)} %get-tuple-element.373, f32[1024,8]{0,1:T(8,128)S(1)} %get-tuple-element.354, pred[]{:T(512)S(6)} %compare.25, f32[1024,1024,8]{1,0,2:T(8,128)} %get-tuple-element.352, f32[1024,8]{0,1:T(8,128)S(1)} %select_maximum_fusion.2, ...), kind=kOutput, calls=%fused_computation.10.clone.1 | convolution fusion | flops 2192572416 | bytes 43319300 | tf_op jit(solution)/shard_map/while/body/eval_jaxpr/thk,dk->thd/dot_general | solution.py:37
  115.4 1.2 compare_and_fusion.2
  116.6 14.9 %fusion.51 = (f32[1024,8]{0,1:T(8,128)S(1)}, f32[1024,1024,8]{1,0,2:T(8,128)}) fusion(pred[1024,1024]{0,1:T(8,128)(4,1)S(1)} %compare_and_fusion.2, bf16[1024,8,128]{2,0,1:T(8,128)(2,1)} %get-tuple-element.394, bf16[128,4096]{0,1:T(8,128)(2,1)} %get-tuple-element.393, s32[]{:T(128)S(6)} %select_n.212), kind=kOutput, calls=%fused_computation.4.clone.1 | convolution fusion | flops 2172641280 | bytes 36995076 | tf_op jit(solution)/shard_map/while/body/eval_jaxpr/thd,dk->thk/dot_general | solution.py:29
  131.4 14.7 %fusion.52 = f32[1024,8]{0,1:T(8,128)S(1)} fusion(f32[1024,1024,8]{1,0,2:T(8,128)} %get-tuple-element.352, f32[1024,8]{0,1:T(8,128)S(1)} %select_maximum_fusion.2, pred[1024,1024]{0,1:T(8,128)(4,1)S(1)} %compare_and_fusion.2), kind=kLoop, calls=%fused_computation.6.clone.1 | loop fusion | flops 41934848 | bytes 34668544 | tf_op jit(solution)/shard_map/while/body/eval_jaxpr/reduce_sum | solution.py:36
  146.2 18.4 %fusion.54 = f32[1024,8,128]{2,0,1:T(8,128)} fusion(f32[1024,8,128]{2,0,1:T(8,128)} %get-tuple-element.373, f32[1024,8]{0,1:T(8,128)S(1)} %get-tuple-element.354, pred[]{:T(512)S(6)} %compare.25, f32[1024,1024,8]{1,0,2:T(8,128)} %get-tuple-element.352, f32[1024,8]{0,1:T(8,128)S(1)} %select_maximum_fusion.2, ...), kind=kOutput, calls=%fused_computation.10.clone.1 | convolution fusion | flops 2192572416 | bytes 43319300 | tf_op jit(solution)/shard_map/while/body/eval_jaxpr/thk,dk->thd/dot_general | solution.py:37
  164.6 1.2 compare_and_fusion.2
  165.8 14.9 %fusion.51 = (f32[1024,8]{0,1:T(8,128)S(1)}, f32[1024,1024,8]{1,0,2:T(8,128)}) fusion(pred[1024,1024]{0,1:T(8,128)(4,1)S(1)} %compare_and_fusion.2, bf16[1024,8,128]{2,0,1:T(8,128)(2,1)} %get-tuple-element.394, bf16[128,4096]{0,1:T(8,128)(2,1)} %get-tuple-element.393, s32[]{:T(128)S(6)} %select_n.212), kind=kOutput, calls=%fused_computation.4.clone.1 | convolution fusion | flops 2172641280 | bytes 36995076 | tf_op jit(solution)/shard_map/while/body/eval_jaxpr/thd,dk->thk/dot_general | solution.py:29
  180.7 14.7 %fusion.52 = f32[1024,8]{0,1:T(8,128)S(1)} fusion(f32[1024,1024,8]{1,0,2:T(8,128)} %get-tuple-element.352, f32[1024,8]{0,1:T(8,128)S(1)} %select_maximum_fusion.2, pred[1024,1024]{0,1:T(8,128)(4,1)S(1)} %compare_and_fusion.2), kind=kLoop, calls=%fused_computation.6.clone.1 | loop fusion | flops 41934848 | bytes 34668544 | tf_op jit(solution)/shard_map/while/body/eval_jaxpr/reduce_sum | solution.py:36
  195.4 18.4 %fusion.54 = f32[1024,8,128]{2,0,1:T(8,128)} fusion(f32[1024,8,128]{2,0,1:T(8,128)} %get-tuple-element.373, f32[1024,8]{0,1:T(8,128)S(1)} %get-tuple-element.354, pred[]{:T(512)S(6)} %compare.25, f32[1024,1024,8]{1,0,2:T(8,128)} %get-tuple-element.352, f32[1024,8]{0,1:T(8,128)S(1)} %select_maximum_fusion.2, ...), kind=kOutput, calls=%fused_computation.10.clone.1 | convolution fusion | flops 2192572416 | bytes 43319300 | tf_op jit(solution)/shard_map/while/body/eval_jaxpr/thk,dk->thd/dot_general | solution.py:37
  213.8 1.2 compare_and_fusion.2
  215.0 14.9 %fusion.51 = (f32[1024,8]{0,1:T(8,128)S(1)}, f32[1024,1024,8]{1,0,2:T(8,128)}) fusion(pred[1024,1024]{0,1:T(8,128)(4,1)S(1)} %compare_and_fusion.2, bf16[1024,8,128]{2,0,1:T(8,128)(2,1)} %get-tuple-element.394, bf16[128,4096]{0,1:T(8,128)(2,1)} %get-tuple-element.393, s32[]{:T(128)S(6)} %select_n.212), kind=kOutput, calls=%fused_computation.4.clone.1 | convolution fusion | flops 2172641280 | bytes 36995076 | tf_op jit(solution)/shard_map/while/body/eval_jaxpr/thd,dk->thk/dot_general | solution.py:29
  229.9 14.7 %fusion.52 = f32[1024,8]{0,1:T(8,128)S(1)} fusion(f32[1024,1024,8]{1,0,2:T(8,128)} %get-tuple-element.352, f32[1024,8]{0,1:T(8,128)S(1)} %select_maximum_fusion.2, pred[1024,1024]{0,1:T(8,128)(4,1)S(1)} %compare_and_fusion.2), kind=kLoop, calls=%fused_computation.6.clone.1 | loop fusion | flops 41934848 | bytes 34668544 | tf_op jit(solution)/shard_map/while/body/eval_jaxpr/reduce_sum | solution.py:36
  244.6 18.4 %fusion.54 = f32[1024,8,128]{2,0,1:T(8,128)} fusion(f32[1024,8,128]{2,0,1:T(8,128)} %get-tuple-element.373, f32[1024,8]{0,1:T(8,128)S(1)} %get-tuple-element.354, pred[]{:T(512)S(6)} %compare.25, f32[1024,1024,8]{1,0,2:T(8,128)} %get-tuple-element.352, f32[1024,8]{0,1:T(8,128)S(1)} %select_maximum_fusion.2, ...), kind=kOutput, calls=%fused_computation.10.clone.1 | convolution fusion | flops 2192572416 | bytes 43319300 | tf_op jit(solution)/shard_map/while/body/eval_jaxpr/thk,dk->thd/dot_general | solution.py:37
  263.0 5.5 %copy.18 = f32[1024,8,128]{0,2,1:T(8,128)} copy(f32[1024,8,128]{2,0,1:T(8,128)} %get-tuple-element.190) | data formatting | bytes 8388608 | tf_op jit(solution)/shard_map/while | solution.py:65
  268.6 2.8 divide_convert_fusion
  271.4 26.2 %convolution_convert_fusion = bf16[1024,8192]{1,0:T(8,128)(2,1)} fusion(bf16[1024,1024]{0,1:T(8,128)(2,1)S(1)} %bitcast.43, bf16[1024,8192]{1,0:T(8,128)(2,1)} %param.11), kind=kOutput, calls=%fused_computation.26 | convolution fusion | flops 17188257792 | bytes 35651584 | tf_op jit(solution)/shard_map/dot_general | solution.py:100
  297.5 0.0 copy-start.1
  297.5 0.0 reduce-scatter.2.cloned.1.call-update
  297.6 168.4 %reduce-scatter.2.cloned.1.call-done = bf16[1024,1024]{1,0:T(8,128)(2,1)} async-done(((bf16[1024,8192]{1,0:T(8,128)(2,1)}), bf16[1024,1024]{1,0:T(8,128)(2,1)}) %reduce-scatter.2.cloned.1.call-update) | async-done | bytes 2097168 | tf_op jit(solution)/shard_map/reduce_scatter | solution.py:101
  466.0 0.0 copy-done.1
  (34 shorter events, 0.3 us)
Async XLA Ops:
  6.5 1.6 copy-start
  6.5 11.7 %copy-start.2 = (s32[4096]{0:T(1024)S(1)}, s32[4096]{0:T(1024)}, u32[]{:S(2)}) copy-start(s32[4096]{0:T(1024)} %param.13) | copy-start | bytes 49156
  6.5 40.1 %all-gather.3.cloned.1.call-start = ((), (), s32[]{:S(2)}) async-start(), calls=%async_computation.1 | async-start | bytes 1310720 | tf_op jit(solution)/shard_map/all_gather | solution.py:91
  9.0 58.1 %all-gather.5.cloned.1.call-start = ((), (), s32[]{:S(2)}) async-start(), calls=%async_computation.2 | async-start | bytes 1310720 | tf_op jit(solution)/shard_map/all_gather | solution.py:92
  10.8 455.2 %reduce-scatter.2.cloned.1.call-start = ((), (), s32[]{:S(2)}) async-start(), calls=%async_computation.3 | async-start | bytes 18874368 | tf_op jit(solution)/shard_map/reduce_scatter | solution.py:101
  297.5 168.4 %copy-start.1 = (bf16[1024,1024]{1,0:T(8,128)(2,1)S(1)}, bf16[1024,1024]{1,0:T(8,128)(2,1)}, u32[]{:S(2)}) copy-start(bf16[1024,1024]{1,0:T(8,128)(2,1)} %param.9) | copy-start | bytes 6291460
Sparse Core Ops, SparseCore 0:
  9.2 29.3 all-gather.2
  40.4 26.6 all-gather.4
  297.7 168.2 reduce-scatter.1
where the time goes:
time: 474 us; the launch traced here: 472 us
  waiting for transfers between devices  189 us (40%)
  matrix products  158 us (33%)
  other arithmetic  68.1 us (14%)
  local copies, waits for them, and re-layouts  43.7 us (9%)
  between operations  13.3 us (3%)
    reduce_scatter x1, waiting for transfers between devices, shards(): lax.psum_scatter(partial_sum.astype(jnp.bfloat16), 'head', scatter_dimens...  168 us
    dot_general x4, matrix products, attend_block(): jnp.einsum('thk,dk->thd', weights.astype(jnp.bfloat16), value_block, pref...  72.6 us
    dot_general x4, matrix products, attend_block(): jnp.einsum('thd,dk->thk', query_heads, key_block, preferred_element_type=...  59.5 us
    reduce_sum x4, other arithmetic, attend_block(): row_total = row_total * factor + jnp.sum(weights, axis=2)  58.8 us
    gather x2, local copies, waits for them, and re-layouts, locate(): return (places, jnp.take(doc_ids, places))  28.8 us
    dot_general x1, matrix products, shards(): jnp.dot(context, out_weight, preferred_element_type=jnp.float32)  26.2 us
    all_gather x1, waiting for transfers between devices, shards(): lax.all_gather(value_part, 'ctx', axis=1, tiled=True)  20.5 us
  transfers between devices with their start and end apart: 3, of which 2 were waited for; matrix products, arithmetic and copies ran while one was open for 8% of the time, Pallas kernels for 0%

commit v1 on v0

--- a/solution.py
+++ b/solution.py
@@ -6,6 +6,19 @@
 KVH = 8
 HD = 128
 floor_score = -1e30
+
+
+def gather_around(x, axis, dim):
+    ways = lax.axis_size(axis)
+    up = [(d, (d + 1) % ways) for d in range(ways)]
+    down = [(d, (d - 1) % ways) for d in range(ways)]
+    earlier, later = ([x], [x])
+    for _ in range(ways // 2):
+        earlier.append(lax.ppermute(earlier[-1], axis, up))
+    for _ in range((ways - 1) // 2):
+        later.append(lax.ppermute(later[-1], axis, down))
+    line = jnp.concatenate([*earlier[::-1], *later[1:]], axis=dim)
+    return jnp.roll(line, (lax.axis_index(axis) - ways // 2) * x.shape[dim], axis=dim)
 
 
 def locate(row_ids, block_order, doc_ids):
@@ -89,7 +102,7 @@
             jnp.zeros((row_count, head_count, HD), jnp.float32),
         ),
         lax.all_gather(key_part, "ctx", axis=1, tiled=True),
-        lax.all_gather(value_part, "ctx", axis=1, tiled=True),
+        gather_around(value_part, "ctx", 1),
         query_heads,
         query_place,
         query_doc,

time: 474 us -> 460 us (0.970)
  waiting for transfers between devices: 189 us -> 169 us
  starting transfers between devices: 0.09 us -> 6.01 us
    all_gather x1 -> x0, waiting for transfers between devices: 20.5 us -> none  [shards(): lax.all_gather(value_part, 'ctx', axis=1, tiled=True)]
    ppermute x0 -> x3, starting transfers between devices: none -> 5.97 us  [the longest x1 3.95 us: gather_around(): later.append(lax.ppermute(later[-1], axis, down))]
  transfers between devices with their start and end apart: 3 -> 5, of which waited for: 2 -> 1; matrix products, arithmetic and copies ran while one was open for 8% -> 9% of each run, Pallas kernels for 0% -> 0%
where the time goes in v1:
time: 460 us; the launch traced here: 459 us
  waiting for transfers between devices  169 us (37%)
  matrix products  158 us (34%)
  other arithmetic  68.1 us (15%)
  local copies, waits for them, and re-layouts  44 us (10%)
  between operations  13.6 us (3%)
  starting transfers between devices  6.01 us (1%)
    reduce_scatter x1, waiting for transfers between devices, shards(): lax.psum_scatter(partial_sum.astype(jnp.bfloat16), 'head', scatter_dimens...  169 us
    dot_general x4, matrix products, attend_block(): jnp.einsum('thk,dk->thd', weights.astype(jnp.bfloat16), value_block, pref...  72.3 us
    dot_general x4, matrix products, attend_block(): jnp.einsum('thd,dk->thk', query_heads, key_block, preferred_element_type=...  59.5 us
    reduce_sum x4, other arithmetic, attend_block(): row_total = row_total * factor + jnp.sum(weights, axis=2)  58.8 us
    gather x2, local copies, waits for them, and re-layouts, locate(): return (places, jnp.take(doc_ids, places))  29.2 us
    dot_general x1, matrix products, shards(): jnp.dot(context, out_weight, preferred_element_type=jnp.float32)  26.2 us
  transfers between devices with their start and end apart: 5, of which 1 were waited for; matrix products, arithmetic and copies ran while one was open for 9% of the time, Pallas kernels for 0%

profile of v1, /device:TPU:0, one launch (start us, length us, event | category | flops | bytes accessed | tf_op | source)
XLA Modules:
  0.0 458.6 jit_solution(6688580187778084996)
XLA Ops:
  6.5 0.0 copy-start
  6.5 0.0 all-gather.2.cloned.1.call-start
  6.5 1.1 constant_dynamic-slice_fusion
  7.7 3.9 collective-permute-start.2
  11.6 0.0 collective-permute-start
  11.6 0.0 copy-done
  11.6 0.8 copy.20
  12.5 0.0 all-gather.2.cloned.1.call-update
  12.5 0.0 reduce-scatter.2.cloned.1.call-start
  12.6 0.7 select_reduce_fusion.1
  13.3 0.8 select_reduce_fusion
  14.2 0.0 copy-done.2
  14.2 23.0 %gather_fusion = s32[4096]{0:T(1024)S(1)} fusion(s32[4096]{0:T(1024)S(1)} %copy-done.2, s32[4096]{0:T(1024)S(1)} %broadcast_clamp_fusion), kind=kCustom, calls=%fused_computation | custom fusion | bytes 49152 | tf_op jit(solution)/shard_map/jit(_take)/gather | solution.py:32
  37.3 0.0 collective-permute-done
  37.3 2.0 collective-permute-start.1
  39.3 6.1 %gather_fusion.1 = s32[1024]{0:T(1024)S(1)} fusion(s32[4096]{0:T(1024)S(1)} %copy-done.2, s32[1024]{0:T(1024)S(1)} %broadcast_clamp_fusion.1), kind=kCustom, calls=%fused_computation.1 | custom fusion | bytes 12288 | tf_op jit(solution)/shard_map/jit(_take)/gather | solution.py:32
  45.4 2.9 copy.16
  48.3 2.4 copy.17
  50.7 0.0 collective-permute-done.1
  50.8 1.0 constant_dynamic-update-slice_fusion.5
  51.7 0.0 collective-permute-done.2
  51.8 1.0 constant_dynamic-update-slice_fusion.1
  52.8 0.1 constant_dynamic-slice_fusion.2
  53.0 0.0 all-gather.2.cloned.1.call-done
  53.0 195.7 %while.18 = (s32[]{:T(128)}, f32[1024,8]{0,1:T(8,128)S(1)}, f32[1024,8]{0,1:T(8,128)S(1)}, f32[1024,8,128]{2,0,1:T(8,128)}, s32[4096]{0:T(1024)S(1)}, /*index=5*...) while((s32[]{:T(128)}, f32[1024,8]{0,1:T(8,128)S(1)}, ...), condition=%wide.region_5.6_spmd.clone, body=%wide.region_2.5_spmd.clone.sunk | while | flops 4410351616 | bytes 116424928 | solution.py:78
  53.0 1.2 compare_and_fusion.2
  54.2 14.9 %fusion.51 = (f32[1024,8]{0,1:T(8,128)S(1)}, f32[1024,1024,8]{1,0,2:T(8,128)}) fusion(pred[1024,1024]{0,1:T(8,128)(4,1)S(1)} %compare_and_fusion.2, bf16[1024,8,128]{2,0,1:T(8,128)(2,1)} %get-tuple-element.394, bf16[128,4096]{0,1:T(8,128)(2,1)} %get-tuple-element.393, s32[]{:T(128)S(6)} %select_n.226), kind=kOutput, calls=%fused_computation.4.clone.1 | convolution fusion | flops 2172641280 | bytes 36995076 | tf_op jit(solution)/shard_map/while/body/eval_jaxpr/thd,dk->thk/dot_general | solution.py:42
  69.1 14.7 %fusion.52 = f32[1024,8]{0,1:T(8,128)S(1)} fusion(f32[1024,1024,8]{1,0,2:T(8,128)} %get-tuple-element.352, f32[1024,8]{0,1:T(8,128)S(1)} %select_maximum_fusion.2, pred[1024,1024]{0,1:T(8,128)(4,1)S(1)} %compare_and_fusion.2), kind=kLoop, calls=%fused_computation.6.clone.1 | loop fusion | flops 41934848 | bytes 34668544 | tf_op jit(solution)/shard_map/while/body/eval_jaxpr/reduce_sum | solution.py:49
  83.9 17.4 %fusion.54 = f32[1024,8,128]{2,0,1:T(8,128)} fusion(f32[1024,8,128]{2,0,1:T(8,128)} %get-tuple-element.373, f32[1024,8]{0,1:T(8,128)S(1)} %get-tuple-element.354, pred[]{:T(512)S(6)} %compare.26, f32[1024,1024,8]{1,0,2:T(8,128)} %get-tuple-element.352, f32[1024,8]{0,1:T(8,128)S(1)} %select_maximum_fusion.2, ...), kind=kOutput, calls=%fused_computation.10.clone.1 | convolution fusion | flops 2192572416 | bytes 43319300 | tf_op jit(solution)/shard_map/while/body/eval_jaxpr/thk,dk->thd/dot_general | solution.py:50
  101.3 1.2 compare_and_fusion.2
  102.5 14.9 %fusion.51 = (f32[1024,8]{0,1:T(8,128)S(1)}, f32[1024,1024,8]{1,0,2:T(8,128)}) fusion(pred[1024,1024]{0,1:T(8,128)(4,1)S(1)} %compare_and_fusion.2, bf16[1024,8,128]{2,0,1:T(8,128)(2,1)} %get-tuple-element.394, bf16[128,4096]{0,1:T(8,128)(2,1)} %get-tuple-element.393, s32[]{:T(128)S(6)} %select_n.226), kind=kOutput, calls=%fused_computation.4.clone.1 | convolution fusion | flops 2172641280 | bytes 36995076 | tf_op jit(solution)/shard_map/while/body/eval_jaxpr/thd,dk->thk/dot_general | solution.py:42
  117.4 14.7 %fusion.52 = f32[1024,8]{0,1:T(8,128)S(1)} fusion(f32[1024,1024,8]{1,0,2:T(8,128)} %get-tuple-element.352, f32[1024,8]{0,1:T(8,128)S(1)} %select_maximum_fusion.2, pred[1024,1024]{0,1:T(8,128)(4,1)S(1)} %compare_and_fusion.2), kind=kLoop, calls=%fused_computation.6.clone.1 | loop fusion | flops 41934848 | bytes 34668544 | tf_op jit(solution)/shard_map/while/body/eval_jaxpr/reduce_sum | solution.py:49
  132.1 18.3 %fusion.54 = f32[1024,8,128]{2,0,1:T(8,128)} fusion(f32[1024,8,128]{2,0,1:T(8,128)} %get-tuple-element.373, f32[1024,8]{0,1:T(8,128)S(1)} %get-tuple-element.354, pred[]{:T(512)S(6)} %compare.26, f32[1024,1024,8]{1,0,2:T(8,128)} %get-tuple-element.352, f32[1024,8]{0,1:T(8,128)S(1)} %select_maximum_fusion.2, ...), kind=kOutput, calls=%fused_computation.10.clone.1 | convolution fusion | flops 2192572416 | bytes 43319300 | tf_op jit(solution)/shard_map/while/body/eval_jaxpr/thk,dk->thd/dot_general | solution.py:50
  150.4 1.2 compare_and_fusion.2
  151.6 14.9 %fusion.51 = (f32[1024,8]{0,1:T(8,128)S(1)}, f32[1024,1024,8]{1,0,2:T(8,128)}) fusion(pred[1024,1024]{0,1:T(8,128)(4,1)S(1)} %compare_and_fusion.2, bf16[1024,8,128]{2,0,1:T(8,128)(2,1)} %get-tuple-element.394, bf16[128,4096]{0,1:T(8,128)(2,1)} %get-tuple-element.393, s32[]{:T(128)S(6)} %select_n.226), kind=kOutput, calls=%fused_computation.4.clone.1 | convolution fusion | flops 2172641280 | bytes 36995076 | tf_op jit(solution)/shard_map/while/body/eval_jaxpr/thd,dk->thk/dot_general | solution.py:42
  166.5 14.7 %fusion.52 = f32[1024,8]{0,1:T(8,128)S(1)} fusion(f32[1024,1024,8]{1,0,2:T(8,128)} %get-tuple-element.352, f32[1024,8]{0,1:T(8,128)S(1)} %select_maximum_fusion.2, pred[1024,1024]{0,1:T(8,128)(4,1)S(1)} %compare_and_fusion.2), kind=kLoop, calls=%fused_computation.6.clone.1 | loop fusion | flops 41934848 | bytes 34668544 | tf_op jit(solution)/shard_map/while/body/eval_jaxpr/reduce_sum | solution.py:49
  181.3 18.3 %fusion.54 = f32[1024,8,128]{2,0,1:T(8,128)} fusion(f32[1024,8,128]{2,0,1:T(8,128)} %get-tuple-element.373, f32[1024,8]{0,1:T(8,128)S(1)} %get-tuple-element.354, pred[]{:T(512)S(6)} %compare.26, f32[1024,1024,8]{1,0,2:T(8,128)} %get-tuple-element.352, f32[1024,8]{0,1:T(8,128)S(1)} %select_maximum_fusion.2, ...), kind=kOutput, calls=%fused_computation.10.clone.1 | convolution fusion | flops 2192572416 | bytes 43319300 | tf_op jit(solution)/shard_map/while/body/eval_jaxpr/thk,dk->thd/dot_general | solution.py:50
  199.6 1.2 compare_and_fusion.2
  200.8 14.9 %fusion.51 = (f32[1024,8]{0,1:T(8,128)S(1)}, f32[1024,1024,8]{1,0,2:T(8,128)}) fusion(pred[1024,1024]{0,1:T(8,128)(4,1)S(1)} %compare_and_fusion.2, bf16[1024,8,128]{2,0,1:T(8,128)(2,1)} %get-tuple-element.394, bf16[128,4096]{0,1:T(8,128)(2,1)} %get-tuple-element.393, s32[]{:T(128)S(6)} %select_n.226), kind=kOutput, calls=%fused_computation.4.clone.1 | convolution fusion | flops 2172641280 | bytes 36995076 | tf_op jit(solution)/shard_map/while/body/eval_jaxpr/thd,dk->thk/dot_general | solution.py:42
  215.7 14.7 %fusion.52 = f32[1024,8]{0,1:T(8,128)S(1)} fusion(f32[1024,1024,8]{1,0,2:T(8,128)} %get-tuple-element.352, f32[1024,8]{0,1:T(8,128)S(1)} %select_maximum_fusion.2, pred[1024,1024]{0,1:T(8,128)(4,1)S(1)} %compare_and_fusion.2), kind=kLoop, calls=%fused_computation.6.clone.1 | loop fusion | flops 41934848 | bytes 34668544 | tf_op jit(solution)/shard_map/while/body/eval_jaxpr/reduce_sum | solution.py:49
  230.4 18.3 %fusion.54 = f32[1024,8,128]{2,0,1:T(8,128)} fusion(f32[1024,8,128]{2,0,1:T(8,128)} %get-tuple-element.373, f32[1024,8]{0,1:T(8,128)S(1)} %get-tuple-element.354, pred[]{:T(512)S(6)} %compare.26, f32[1024,1024,8]{1,0,2:T(8,128)} %get-tuple-element.352, f32[1024,8]{0,1:T(8,128)S(1)} %select_maximum_fusion.2, ...), kind=kOutput, calls=%fused_computation.10.clone.1 | convolution fusion | flops 2192572416 | bytes 43319300 | tf_op jit(solution)/shard_map/while/body/eval_jaxpr/thk,dk->thd/dot_general | solution.py:50
  248.7 5.3 %copy.18 = f32[1024,8,128]{0,2,1:T(8,128)} copy(f32[1024,8,128]{2,0,1:T(8,128)} %get-tuple-element.190) | data formatting | bytes 8388608 | tf_op jit(solution)/shard_map/while | solution.py:78
  254.1 2.8 divide_convert_fusion
  256.9 26.2 %convolution_convert_fusion = bf16[1024,8192]{1,0:T(8,128)(2,1)} fusion(bf16[1024,1024]{0,1:T(8,128)(2,1)S(1)} %bitcast.43, bf16[1024,8192]{1,0:T(8,128)(2,1)} %param.11), kind=kOutput, calls=%fused_computation.26 | convolution fusion | flops 17188257792 | bytes 35651584 | tf_op jit(solution)/shard_map/dot_general | solution.py:113
  283.0 0.0 reduce-scatter.2.cloned.1.call-update
  283.1 0.0 copy-start.1
  283.1 168.7 %reduce-scatter.2.cloned.1.call-done = bf16[1024,1024]{1,0:T(8,128)(2,1)} async-done(((bf16[1024,8192]{1,0:T(8,128)(2,1)}), bf16[1024,1024]{1,0:T(8,128)(2,1)}) %reduce-scatter.2.cloned.1.call-update) | async-done | bytes 2097168 | tf_op jit(solution)/shard_map/reduce_scatter | solution.py:114
  451.8 0.0 copy-done.1
  (41 shorter events, 0.4 us)
Async XLA Ops:
  6.5 5.1 %copy-start = (bf16[1024,1024]{1,0:T(8,128)(2,1)S(1)}, bf16[1024,1024]{1,0:T(8,128)(2,1)}, u32[]{:S(2)}) copy-start(bf16[1024,1024]{1,0:T(8,128)(2,1)} %param.9) | copy-start | bytes 6291460
  6.5 7.6 %copy-start.2 = (s32[4096]{0:T(1024)S(1)}, s32[4096]{0:T(1024)}, u32[]{:S(2)}) copy-start(s32[4096]{0:T(1024)} %param.13) | copy-start | bytes 49156
  6.5 46.4 %all-gather.2.cloned.1.call-start = ((), (), s32[]{:S(2)}) async-start(), calls=%async_computation.1 | async-start | bytes 1310720 | tf_op jit(solution)/shard_map/all_gather | solution.py:104
  7.7 44.1 %collective-permute-start.2 = (bf16[128,1024]{1,0:T(8,128)(2,1)S(1)}, bf16[128,1024]{1,0:T(8,128)(2,1)S(1)}, u32[]{:S(2)}, u32[]{:S(2)}) collective-permute-start(bf16[128,1024]{1,0:T(8,128)(2,1)S(1)} %constant_dynamic-slice_fusion), channel_id=1, source_target_pairs={{0,24},{8,0},{16,8},{24,16},{1,25},{9,1},{17,9},{25,17},{2,26},{10... | collective-permute-start | bytes 786440 | tf_op jit(solution)/shard_map/ppermute | solution.py:19
  11.6 25.6 %collective-permute-start = (bf16[128,1024]{1,0:T(8,128)(2,1)S(1)}, bf16[128,1024]{1,0:T(8,128)(2,1)S(1)}, u32[]{:S(2)}, u32[]{:S(2)}) collective-permute-start(bf16[128,1024]{1,0:T(8,128)(2,1)S(1)} %constant_dynamic-slice_fusion), channel_id=1, source_target_pairs={{0,8},{8,16},{16,24},{24,0},{1,9},{9,17},{17,25},{25,1},{2,10},{10... | collective-permute-start | bytes 786440 | tf_op jit(solution)/shard_map/ppermute | solution.py:17
  12.5 439.3 %reduce-scatter.2.cloned.1.call-start = ((), (), s32[]{:S(2)}) async-start(), calls=%async_computation.2 | async-start | bytes 18874368 | tf_op jit(solution)/shard_map/reduce_scatter | solution.py:114
  37.3 13.4 %collective-permute-start.1 = (bf16[128,1024]{1,0:T(8,128)(2,1)S(1)}, bf16[128,1024]{1,0:T(8,128)(2,1)S(1)}, u32[]{:S(2)}, u32[]{:S(2)}) collective-permute-start(bf16[128,1024]{1,0:T(8,128)(2,1)S(1)} %collective-permute-done), channel_id=1, source_target_pairs={{0,8},{8,16},{16,24},{24,0},{1,9},{9,17},{17,25},{25,1},{2,10},{10... | collective-permute-start | bytes 786440 | tf_op jit(solution)/shard_map/ppermute | solution.py:17
  283.1 168.7 %copy-start.1 = (bf16[1024,1024]{1,0:T(8,128)(2,1)S(1)}, bf16[1024,1024]{1,0:T(8,128)(2,1)}, u32[]{:S(2)}) copy-start(bf16[1024,1024]{1,0:T(8,128)(2,1)} %param.9) | copy-start | bytes 6291460
Sparse Core Ops, SparseCore 0:
  12.6 28.9 all-gather.1
  283.2 168.5 reduce-scatter.1
